TPU v7x, 512 devices: a whole 4x8x8 slice. The times are simulated.
512 devices in a mesh: shard: 64 (over x, z, core), tensor: 8 (over y).
Axes of the slice: x: 4, y: 8, z: 8, core: 2. Of those that a mesh axis runs over, the one named last changes fastest.
Arguments:
- grad: float32 [8, 512, 1024], P(None, 'shard', 'tensor'), may hold values from -500 to 500
- momentum: float32 [8, 512, 1024], P(None, 'shard', 'tensor'), may hold values from -6 to 6
- weight: float32 [8, 512, 1024], P(None, 'shard', 'tensor'), may hold values from -0.625 to 0.625
Outputs:
- new_weight: float32 [8, 512, 1024], P(None, 'shard', 'tensor')
- new_momentum: float32 [8, 512, 1024], P(None, 'shard', 'tensor')
- update: float32 [8, 512, 1024], P(None, 'shard', 'tensor')
All inputs are finite; a program needn't handle non-finite values.
Results may differ from a plain program's by a relative error of at most 0.0078.
Values may be sent and summed in bfloat16 or wider, within the bound.
A program may use at most 64 MiB of HBM per device.

v0:
```python
import math
import jax
import jax.numpy as jnp
from jax import lax
from jax.sharding import PartitionSpec as P

ITERS = 3
mu_decay = 0.95
learn_rate = 0.05
weight_decay = 0.1
update_gain = 0.2
first_coef = 3.4445
second_coef = -4.775
third_coef = 2.0315
epsilon = 1e-07


def regroup(values):
    return lax.all_to_all(
        lax.all_to_all(values, "shard", split_axis=3, concat_axis=1, tiled=True),
        "tensor",
        split_axis=0,
        concat_axis=2,
        tiled=True,
    )


def polish(iterate, gram):
    wide = iterate.astype(jnp.float32)
    squared = jnp.einsum("mrs,mst->mrt", gram, gram, precision=lax.Precision.HIGHEST)
    poly = second_coef * gram + third_coef * squared
    mixed = jnp.einsum("mrs,msc->mrc", poly, wide, precision=lax.Precision.HIGHEST)
    fresh = first_coef * wide + mixed
    return fresh.astype(jnp.bfloat16)


def on_device(grad, momentum, weight):
    mats, rows_local, cols_local = grad.shape
    n_shard = lax.axis_size("shard")
    n_tensor = lax.axis_size("tensor")
    new_momentum = mu_decay * momentum + grad
    advance = lax.optimization_barrier((grad + mu_decay * new_momentum).astype(jnp.bfloat16))
    wide = advance.astype(jnp.float32)
    total = lax.psum(jnp.sum(wide * wide, axis=(1, 2)), ("shard", "tensor"))
    frob = jnp.sqrt(total)[:, None, None] + epsilon
    start = (wide / frob).astype(jnp.bfloat16)
    moved = regroup(start.reshape(mats, rows_local, 1, cols_local))
    group, kv_rows, tensor_cols, thin_cols = moved.shape
    gathered = lax.all_gather(moved, "shard", axis=3, tiled=True)
    iterate = gathered.reshape(group, kv_rows, tensor_cols * n_shard * thin_cols)
    for step in range(ITERS):
        gram = jnp.einsum("mrc,msc->mrs", iterate, iterate, preferred_element_type=jnp.float32)
        iterate = polish(iterate, gram)
    spread = iterate.reshape(group, kv_rows, tensor_cols, n_shard, thin_cols)
    result = lax.dynamic_index_in_dim(spread, lax.axis_index("shard"), 3, keepdims=False)
    back = lax.all_to_all(
        lax.all_to_all(result, "shard", split_axis=1, concat_axis=3, tiled=True),
        "tensor",
        split_axis=2,
        concat_axis=0,
        tiled=True,
    )
    ortho = back.reshape(mats, rows_local, cols_local)
    width = cols_local * n_tensor
    update = update_gain * math.sqrt(width) * ortho.astype(jnp.float32)
    new_weight = weight - learn_rate * (update + weight_decay * weight)
    return (new_weight, new_momentum, update)


def solution(mesh):
    in_specs = (P(None, "shard", "tensor"), P(None, "shard", "tensor"), P(None, "shard", "tensor"))
    out_specs = (P(None, "shard", "tensor"), P(None, "shard", "tensor"), P(None, "shard", "tensor"))
    return jax.shard_map(
        on_device, mesh=mesh, in_specs=in_specs, out_specs=out_specs, check_vma=False
    )
```

profile of v0, /device:TPU:6, one launch (start us, length us, event | category | flops | bytes accessed | tf_op | source)
XLA Modules:
  0.0 277.9 jit_solution(15786168088153653814)
XLA Ops:
  7.2 1.4 add_convert_fusion.3
  8.7 103.3 %psum.7 = f32[8]{0:T(128)S(1)} all-reduce(f32[8]{0:T(128)S(1)} %fusion.4), channel_id=1, replica_groups=mesh['shard'=64,'tensor'=8] {'shard','tensor'}, use_global_device_ids=true, to_apply=%region_1.0 | all-reduce | flops 8 | bytes 64 | tf_op jit(solution)/shard_map/psum | solution.py:44
  112.4 17.5 %all_to_all.63 = bf16[8,8,1,128]{1,0,2,3:T(8,128)(2,1)S(1)} all-to-all(bf16[8,8,1,128]{1,0,2,3:T(8,128)(2,1)S(1)} %copy.53), channel_id=1, replica_groups=mesh['shard'=64,'tensor'=8] {'shard'}, dimensions={3} | all-to-all | bytes 32768 | tf_op jit(solution)/shard_map/all_to_all | solution.py:20
  130.3 13.0 %all_to_all.64 = bf16[8,512,1,2]{1,3,2,0:T(2,128)(2,1)S(1)} all-to-all(bf16[8,512,1,2]{1,3,2,0:T(2,128)(2,1)S(1)} %reshape.105), channel_id=1, replica_groups=mesh['shard'=64,'tensor'=8] {'tensor'}, dimensions={0} | all-to-all | bytes 32768 | tf_op jit(solution)/shard_map/all_to_all | solution.py:19
  143.2 0.6 copy.56
  143.9 74.2 %all-gather.3.cloned.1.call-done = bf16[1,512,8,1,128]{1,2,3,0,4:T(8,128)(2,1)} async-done(((bf16[1,512,8,1,2]{1,2,3,0,4:T(8,128)(2,1)}), bf16[1,512,8,1,128]{1,2,3,0,4:T(8,128)(2,1)}) %all-gather.3.cloned.1.call-update) | async-done | bytes 1048592 | tf_op jit(solution)/shard_map/all_gather | solution.py:49
  218.0 1.9 copy.59
  220.0 0.7 convolution_bitcast_fusion
  220.7 1.9 fusion.2
  222.9 0.7 copy.58
  223.7 1.9 add_convert_fusion.2
  225.5 0.7 fusion.7
  226.3 1.9 fusion.1
  228.2 1.9 add_convert_fusion.1
  230.1 0.7 fusion.8
  230.8 1.9 fusion
  232.7 1.9 add_convert_fusion
  234.6 0.5 copy.60
  235.2 0.4 reshape.100
  235.8 19.2 %all_to_all.65 = bf16[1,512,8,2]{2,3,0,1:T(2,128)(2,1)S(1)} all-to-all(bf16[1,512,8,2]{2,3,0,1:T(2,128)(2,1)S(1)} %copy.62), channel_id=1, replica_groups=mesh['shard'=64,'tensor'=8] {'shard'}, dimensions={1} | all-to-all | bytes 32768 | tf_op jit(solution)/shard_map/all_to_all | solution.py:57
  255.1 0.5 copy.69
  255.6 0.4 copy.64
  256.1 14.3 %all_to_all.66 = bf16[1,8,8,128]{3,1,0,2:T(8,128)(2,1)S(1)} all-to-all(bf16[1,8,8,128]{3,1,0,2:T(8,128)(2,1)S(1)} %copy.65), channel_id=1, replica_groups=mesh['shard'=64,'tensor'=8] {'tensor'}, dimensions={2} | all-to-all | bytes 32768 | tf_op jit(solution)/shard_map/all_to_all | solution.py:56
  270.4 0.6 multiply_subtract_fusion
  (16 shorter events, 1.5 us)
Async XLA Ops:
  7.2 210.9 %all-gather.3.cloned.1.call-start = ((), (), s32[]{:S(2)}) async-start(), calls=%async_computation.4 | async-start | bytes 1064960 | tf_op jit(solution)/shard_map/all_gather | solution.py:49
  220.7 1.9 copy-start
  235.6 34.8 %copy-start.1 = (f32[8,8,128]{2,1,0:T(8,128)S(1)}, f32[8,8,128]{2,1,0:T(8,128)}, u32[]{:S(2)}) copy-start(f32[8,8,128]{2,1,0:T(8,128)} %param.5) | copy-start | bytes 98308
Sparse Core Ops, SparseCore 0:
  144.0 74.0 all-gather.2
where the time goes:
time: 278 us
  blocking collectives  167 us (60%)
  waiting for transfers between devices  74.2 us (27%)
  between operations  14.2 us (5%)
  matrix products  13.5 us (5%)
  local copies, waits for them, and re-layouts  6.34 us (2%)
    psum x1, blocking collectives, on_device(): total = lax.psum(jnp.sum(wide * wide, axis=(1, 2)), ('shard', 'tensor'))  103 us
    all_gather x1, waiting for transfers between devices, on_device(): gathered = lax.all_gather(moved, 'shard', axis=3, tiled=True)  74.2 us
    all_to_all x1, blocking collectives, on_device(): lax.all_to_all(result, 'shard', split_axis=1, concat_axis=3, tiled=True)  19.2 us
    all_to_all x1, blocking collectives, regroup(): lax.all_to_all(values, 'shard', split_axis=3, concat_axis=1, tiled=True)  17.5 us
    all_to_all x1, blocking collectives, on_device(): lax.all_to_all(lax.all_to_all(result, 'shard', split_axis=1, concat_axis=...  14.3 us
    all_to_all x1, blocking collectives, regroup(): lax.all_to_all(lax.all_to_all(values, 'shard', split_axis=3, concat_axis=...  13 us
    dot_general x3, matrix products, polish(): jnp.einsum('mrs,mst->mrt', gram, gram, precision=lax.Precision.HIGHEST)  5.7 us
    dot_general x3, matrix products, polish(): jnp.einsum('mrs,msc->mrc', poly, wide, precision=lax.Precision.HIGHEST)  5.58 us
  transfers between devices with their start and end apart: 1, of which 1 were waited for; matrix products, arithmetic and copies ran while one was open for 0% of the time, Pallas kernels for 0%

commit v1 on v0

--- a/solution.py
+++ b/solution.py
@@ -46,7 +46,16 @@
     start = (wide / frob).astype(jnp.bfloat16)
     moved = regroup(start.reshape(mats, rows_local, 1, cols_local))
     group, kv_rows, tensor_cols, thin_cols = moved.shape
-    gathered = lax.all_gather(moved, "shard", axis=3, tiled=True)
+    define_sums_all = lambda s0, row_axis, on_dim: jnp.concatenate(
+        lax.all_to_all(
+            jnp.stack([s0 for _ in range(lax.axis_size(row_axis))], axis=0),
+            axis_name=row_axis,
+            split_axis=0,
+            concat_axis=0,
+        ),
+        on_dim,
+    )
+    gathered = define_sums_all(moved, "shard", 3)
     iterate = gathered.reshape(group, kv_rows, tensor_cols * n_shard * thin_cols)
     for step in range(ITERS):
         gram = jnp.einsum("mrc,msc->mrs", iterate, iterate, preferred_element_type=jnp.float32)

time: 278 us -> 222 us (0.80)
  waiting for transfers between devices: 74.2 us -> 26.6 us
  between operations: 14.2 us -> 0.8 us
  starting transfers between devices: 0.04 us -> 6.46 us
  blocking collectives: 167 us -> 163 us
    all_gather x1 -> x0, waiting for transfers between devices: 74.2 us -> none  [on_device(): gathered = lax.all_gather(moved, 'shard', axis=3, tiled=True)]
    all_to_all x0 -> x1, waiting for transfers between devices: none -> 26.6 us  [on_device(): lax.all_to_all(jnp.stack([s0 for _ in range(lax.axis_size(row_axis))], ax...]
    all_to_all x0 -> x1, starting transfers between devices: none -> 6.46 us  [on_device(): lax.all_to_all(jnp.stack([s0 for _ in range(lax.axis_size(row_axis))], ax...]
    all_to_all x1, blocking collectives: 14.3 us -> 10.1 us  [on_device(): lax.all_to_all(lax.all_to_all(result, 'shard', split_axis=1, concat_axis=...]
    another operation x0 -> x3, local copies, waits for them, and re-layouts: none -> 3.16 us  [the longest x1 2 us: on_device(): jnp.stack([s0 for _ in range(lax.axis_size(row_axis))], axis=0)]
where the time goes in v1:
time: 222 us
  blocking collectives  163 us (73%)
  waiting for transfers between devices  26.6 us (12%)
  matrix products  14.7 us (7%)
  local copies, waits for them, and re-layouts  7.58 us (3%)
  starting transfers between devices  6.46 us (3%)
  other arithmetic  2.27 us (1%)
    psum x1, blocking collectives, on_device(): total = lax.psum(jnp.sum(wide * wide, axis=(1, 2)), ('shard', 'tensor'))  103 us
    all_to_all x1, waiting for transfers between devices, on_device(): lax.all_to_all(jnp.stack([s0 for _ in range(lax.axis_size(row_axis))], ax...  26.6 us
    all_to_all x1, blocking collectives, on_device(): lax.all_to_all(result, 'shard', split_axis=1, concat_axis=3, tiled=True)  19.4 us
    all_to_all x1, blocking collectives, regroup(): lax.all_to_all(values, 'shard', split_axis=3, concat_axis=1, tiled=True)  17.5 us
    all_to_all x1, blocking collectives, regroup(): lax.all_to_all(lax.all_to_all(values, 'shard', split_axis=3, concat_axis=...  13 us
    all_to_all x1, blocking collectives, on_device(): lax.all_to_all(lax.all_to_all(result, 'shard', split_axis=1, concat_axis=...  10.1 us
    all_to_all x1, starting transfers between devices, on_device(): lax.all_to_all(jnp.stack([s0 for _ in range(lax.axis_size(row_axis))], ax...  6.46 us
    dot_general x3, matrix products, polish(): jnp.einsum('mrs,mst->mrt', gram, gram, precision=lax.Precision.HIGHEST)  5.7 us
  transfers between devices with their start and end apart: 1, of which 1 were waited for; matrix products, arithmetic and copies ran while one was open for 0% of the time, Pallas kernels for 0%

profile of v1, /device:TPU:6, one launch (start us, length us, event | category | flops | bytes accessed | tf_op | source)
XLA Modules:
  0.0 221.9 jit_solution(9073263057486580648)
XLA Ops:
  0.6 1.4 add_convert_fusion.3
  2.2 103.3 %psum.7 = f32[8]{0:T(128)S(1)} all-reduce(f32[8]{0:T(128)S(1)} %fusion.5), channel_id=1, replica_groups=mesh['shard'=64,'tensor'=8] {'shard','tensor'}, use_global_device_ids=true, to_apply=%region_1.0 | all-reduce | flops 8 | bytes 64 | tf_op jit(solution)/shard_map/psum | solution.py:44
  105.8 17.5 %all_to_all.65 = bf16[8,8,1,128]{1,0,2,3:T(8,128)(2,1)S(1)} all-to-all(bf16[8,8,1,128]{1,0,2,3:T(8,128)(2,1)S(1)} %copy.37), channel_id=1, replica_groups=mesh['shard'=64,'tensor'=8] {'shard'}, dimensions={3} | all-to-all | bytes 32768 | tf_op jit(solution)/shard_map/all_to_all | solution.py:20
  123.7 13.0 %all_to_all.66 = bf16[8,512,1,2]{1,3,2,0:T(2,128)(2,1)S(1)} all-to-all(bf16[8,512,1,2]{1,3,2,0:T(2,128)(2,1)S(1)} %reshape.107), channel_id=1, replica_groups=mesh['shard'=64,'tensor'=8] {'tensor'}, dimensions={0} | all-to-all | bytes 32768 | tf_op jit(solution)/shard_map/all_to_all | solution.py:19
  136.6 2.0 stack.5
  138.6 6.5 %all-to-all-start.2 = ((bf16[64,1,512,8,2]{2,4,3,1,0:T(2,128)(2,1)}), bf16[64,1,512,8,2]{2,4,3,1,0:T(2,128)(2,1)S(1)}, u32[]{:S(2)}, u32[]{:S(2)}) async-start(bf16[64,1,512,8,2]{2,4,3,1,0:T(2,128)(2,1)} %stack.5), calls=%async_computation.2 | async-start | bytes 2097152 | tf_op jit(solution)/shard_map/all_to_all | solution.py:50
  145.1 26.6 %all-to-all-done.2 = bf16[64,1,512,8,2]{2,4,3,1,0:T(2,128)(2,1)S(1)} async-done(((bf16[64,1,512,8,2]{2,4,3,1,0:T(2,128)(2,1)}), bf16[64,1,512,8,2]{2,4,3,1,0:T(2,128)(2,1)S(1)}, u32[]{:S(2)}, u32[]{:S(2)}) %all-to-all-start.2) | async-done | bytes 1048608 | tf_op jit(solution)/shard_map/all_to_all | solution.py:50
  171.7 0.6 copy.60
  172.3 1.1 copy.41
  173.9 2.0 convolution_bitcast_fusion
  175.8 1.9 fusion.2
  177.7 0.7 copy.42
  178.4 1.9 add_convert_fusion.2
  180.3 0.7 fusion.8
  181.0 1.9 fusion.1
  183.0 1.9 add_convert_fusion.1
  184.8 0.7 fusion.9
  185.6 1.9 fusion
  187.5 1.9 add_convert_fusion
  189.4 0.5 copy.43
  190.6 19.4 %all_to_all.67 = bf16[1,512,8,2]{2,3,0,1:T(2,128)(2,1)S(1)} all-to-all(bf16[1,512,8,2]{2,3,0,1:T(2,128)(2,1)S(1)} %copy.45), channel_id=1, replica_groups=mesh['shard'=64,'tensor'=8] {'shard'}, dimensions={1} | all-to-all | bytes 32768 | tf_op jit(solution)/shard_map/all_to_all | solution.py:66
  210.0 0.5 copy.53
  211.1 10.1 %all_to_all.68 = bf16[1,8,8,128]{3,1,0,2:T(8,128)(2,1)S(1)} all-to-all(bf16[1,8,8,128]{3,1,0,2:T(8,128)(2,1)S(1)} %copy.48), channel_id=1, replica_groups=mesh['shard'=64,'tensor'=8] {'tensor'}, dimensions={2} | all-to-all | bytes 32768 | tf_op jit(solution)/shard_map/all_to_all | solution.py:65
  221.2 0.6 multiply_subtract_fusion
  (14 shorter events, 2.4 us)
Async XLA Ops:
  138.6 33.1 %all-to-all-start.2 = ((bf16[64,1,512,8,2]{2,4,3,1,0:T(2,128)(2,1)}), bf16[64,1,512,8,2]{2,4,3,1,0:T(2,128)(2,1)S(1)}, u32[]{:S(2)}, u32[]{:S(2)}) async-start(bf16[64,1,512,8,2]{2,4,3,1,0:T(2,128)(2,1)} %stack.5), calls=%async_computation.2 | async-start | bytes 2097152 | tf_op jit(solution)/shard_map/all_to_all | solution.py:50
  190.4 30.8 %copy-start = (f32[8,8,128]{2,1,0:T(8,128)S(1)}, f32[8,8,128]{2,1,0:T(8,128)}, u32[]{:S(2)}) copy-start(f32[8,8,128]{2,1,0:T(8,128)} %param.5) | copy-start | bytes 98308
